TPU v7x, 32 devices: a whole 2x2x4 slice. The times are simulated.
32 devices in a mesh: row: 4 (over z), col: 4 (over x, core), chol: 2 (over y).
Axes of the slice: x: 2, y: 2, z: 4, core: 2. Of those that a mesh axis runs over, the one named last changes fastest.
Arguments:
- left_vectors: bfloat16 [64, 4608, 1536], P(None, ('col', 'chol'), 'row'), may hold values from -0.75 to 0.75
- right_vectors: bfloat16 [16, 4608, 1536], P(None, ('col', 'chol'), 'row'), may hold values from -0.0234375 to 0.0234375
- amplitudes: bfloat16 [8, 16, 64], replicated, may hold values from -6 to 6
Outputs:
- ladder: float32 [8, 1536, 1536], P('chol', 'row', 'col')
All inputs are finite; a program needn't handle non-finite values.
Results may differ from a plain program's by a relative error of at most 0.0029.
Values may be sent and summed in bfloat16 or wider, within the bound.
No kernel may reach another device: no remote copies, remote signals or barrier semaphores. Data moves between devices by JAX's collectives and lax.ppermute only.
A program may use at most 256 MiB of HBM per device.

v0:
```python
import jax
import jax.numpy as jnp
from jax import lax
from jax.sharding import PartitionSpec as P


def shards(left_vectors, right_vectors, amplitudes):
    pairs, d_block, c_block = amplitudes.shape
    amp_rows = amplitudes.reshape(pairs * d_block, c_block)
    width_a = left_vectors.shape[2]
    right_full = lax.all_gather(right_vectors, "row", axis=2, tiled=True)
    columns = lax.axis_size("col")
    width_b = right_full.shape[2] // columns
    vectors = left_vectors.shape[1]
    halved = jnp.dot(
        amp_rows,
        left_vectors.reshape(c_block, vectors * width_a),
        preferred_element_type=jnp.float32,
    ).astype(jnp.bfloat16)
    halved = halved.reshape(pairs, d_block * vectors, width_a)
    panel = right_full.reshape(d_block * vectors, columns, width_b)
    ladder = jnp.einsum("ika,kcb->ciab", halved, panel, preferred_element_type=jnp.float32)
    ladder = ladder.reshape(columns * pairs, width_a, width_b)
    return lax.psum_scatter(ladder, ("col", "chol"), scatter_dimension=0, tiled=True)


def solution(mesh):
    return jax.shard_map(
        shards,
        mesh=mesh,
        in_specs=(P(None, ("col", "chol"), "row"), P(None, ("col", "chol"), "row"), P()),
        out_specs=P("chol", "row", "col"),
        check_vma=False,
    )
```

profile of v0, /device:TPU:0, one launch (start us, length us, event | category | flops | bytes accessed | tf_op | source)
XLA Modules:
  0.0 779.7 jit_solution(12643023936817732366)
XLA Ops:
  6.5 0.0 copy-start
  6.5 0.0 all-gather.2.cloned.1.call-start
  6.5 0.7 all-gather.2.cloned.1.call-update
  7.3 0.0 reduce-scatter.2.cloned.1.call-start
  7.3 40.3 %copy.11 = bf16[8,8,576,384]{3,1,2,0:T(8,128)(2,1)} copy(bf16[8,8,576,384]{3,2,1,0:T(8,128)(2,1)} %bitcast.23) | data formatting | bytes 56623104
  47.6 0.0 copy-done
  47.6 38.6 %convolution_convert_fusion = bf16[128,221184]{1,0:T(8,128)(2,1)} fusion(bf16[128,64]{1,0:T(8,128)(2,1)S(1)} %bitcast.20, bf16[64,221184]{1,0:T(8,128)(2,1)} %bitcast.21), kind=kOutput, calls=%fused_computation | convolution fusion | flops 3652190208 | bytes 84951040 | tf_op jit(solution)/shard_map/dot_general | solution.py:15
  86.2 50.1 %reshape.17 = bf16[8,9216,384]{2,1,0:T(8,128)(2,1)} reshape(bf16[128,221184]{1,0:T(8,128)(2,1)} %convolution_convert_fusion) | data formatting | bytes 113246208 | tf_op jit(solution)/shard_map/reshape | solution.py:20
  136.3 351.5 %all-gather.2.cloned.1.call-done = bf16[16,576,1536]{2,1,0:T(8,128)(2,1)} async-done(((bf16[16,576,384]{2,1,0:T(8,128)(2,1)}), bf16[16,576,1536]{2,1,0:T(8,128)(2,1)}) %all-gather.2.cloned.1.call-update) | async-done | bytes 28311568 | tf_op jit(solution)/shard_map/all_gather | solution.py:11
  487.8 47.2 %reshape.18 = bf16[9216,4,384]{2,1,0:T(4,128)(2,1)} reshape(bf16[16,576,1536]{2,1,0:T(8,128)(2,1)} %all-gather.2.cloned.1.call-done) | data formatting | bytes 56623104 | tf_op jit(solution)/shard_map/reshape | solution.py:21
  535.0 0.0 copy-start.1
  535.0 100.5 %fusion.4 = f32[4,8,384,384]{3,2,0,1:T(8,128)} fusion(bf16[9216,4,384]{2,1,0:T(4,128)(2,1)} %reshape.18, bf16[8,9216,384]{2,1,0:T(8,128)(2,1)} %reshape.17), kind=kOutput, calls=%fused_computation.5 | convolution fusion | flops 86973087744 | bytes 103809024 | tf_op jit(solution)/shard_map/ika,kcb->ciab/dot_general | solution.py:22
  635.5 12.6 %copy.7 = f32[4,8,384,384]{3,2,1,0:T(8,128)} copy(f32[4,8,384,384]{3,2,0,1:T(8,128)} %fusion.4) | data formatting | bytes 37748736 | tf_op jit(solution)/shard_map/ika,kcb->ciab/transpose | solution.py:22
  648.1 0.0 reduce-scatter.2.cloned.1.call-update
  648.1 124.8 %reduce-scatter.2.cloned.1.call-done = f32[4,384,384]{2,1,0:T(8,128)} async-done(((f32[32,384,384]{2,1,0:T(8,128)}), f32[4,384,384]{2,1,0:T(8,128)}) %reduce-scatter.2.cloned.1.call-update) | async-done | bytes 2359312 | tf_op jit(solution)/shard_map/reduce_scatter | solution.py:24
  772.9 0.0 copy-done.1
Async XLA Ops:
  6.5 41.1 %copy-start = (bf16[8,16,64]{2,1,0:T(8,128)(2,1)S(1)}, bf16[8,16,64]{2,1,0:T(8,128)(2,1)}, u32[]{:S(2)}) copy-start(bf16[8,16,64]{2,1,0:T(8,128)(2,1)} %param.5) | copy-start | bytes 49156
  6.5 481.3 %all-gather.2.cloned.1.call-start = ((), (), s32[]{:S(2)}) async-start(), calls=%async_computation.1 | async-start | bytes 35389440 | tf_op jit(solution)/shard_map/all_gather | solution.py:11
  7.3 765.6 %reduce-scatter.2.cloned.1.call-start = ((), (), s32[]{:S(2)}) async-start(), calls=%async_computation.2 | async-start | bytes 21233664 | tf_op jit(solution)/shard_map/reduce_scatter | solution.py:24
  535.0 237.9 %copy-start.1 = (bf16[8,16,64]{2,1,0:T(8,128)(2,1)S(1)}, bf16[8,16,64]{2,1,0:T(8,128)(2,1)}, u32[]{:S(2)}) copy-start(bf16[8,16,64]{2,1,0:T(8,128)(2,1)} %param.5) | copy-start | bytes 49156
Sparse Core Ops, SparseCore 0:
  8.9 478.8 all-gather.1
  648.3 124.6 reduce-scatter.1
where the time goes:
time: 782 us; the launch traced here: 780 us
  waiting for transfers between devices  477 us (61%)
  local copies, waits for them, and re-layouts  150 us (19%)
  matrix products  139 us (18%)
  between operations  13.4 us (2%)
    all_gather x1, waiting for transfers between devices, shards(): right_full = lax.all_gather(right_vectors, 'row', axis=2, tiled=True)  352 us
    reduce_scatter x1, waiting for transfers between devices, shards(): lax.psum_scatter(ladder, ('col', 'chol'), scatter_dimension=0, tiled=True)  125 us
    dot_general x1, matrix products, shards(): jnp.einsum('ika,kcb->ciab', halved, panel, preferred_element_type=jnp.flo...  101 us
    reshape x1, local copies, waits for them, and re-layouts, shards(): halved = halved.reshape(pairs, d_block * vectors, width_a)  50.1 us
    reshape x1, local copies, waits for them, and re-layouts, shards(): panel = right_full.reshape(d_block * vectors, columns, width_b)  47.2 us
    unnamed x5, local copies, waits for them, and re-layouts  40.3 us
    dot_general x1, matrix products, shards(): jnp.dot(amp_rows, left_vectors.reshape(c_block, vectors * width_a), prefe...  38.6 us
  transfers between devices with their start and end apart: 2, of which 2 were waited for; matrix products, arithmetic and copies ran while one was open for 17% of the time, Pallas kernels for 0%

commit v1 on v0

v1 whole, which is shorter than its diff:
```python
import jax
import jax.numpy as jnp
from jax import lax
from jax.experimental import pallas as pl
from jax.sharding import PartitionSpec as P


LANES = 128


def half_kernel(amp_ref, left_ref, out_ref):
    pairs, block, d_block, _ = out_ref.shape
    amp = amp_ref[...]
    for p in range(block):
        res = jnp.dot(amp, left_ref[p], preferred_element_type=jnp.float32).astype(out_ref.dtype)
        for i in range(pairs):
            out_ref[i, p] = res[i * d_block:(i + 1) * d_block]


def halve(amplitudes, left_t):
    pairs, d_block, c_block = amplitudes.shape
    vectors, _, width = left_t.shape
    block = next(b for b in (16, 12, 8, 6, 4, 3, 2, 1) if vectors % b == 0)
    return pl.pallas_call(
        half_kernel,
        grid=(vectors // block,),
        in_specs=[
            pl.BlockSpec((pairs * d_block, c_block), lambda p: (0, 0)),
            pl.BlockSpec((block, c_block, width), lambda p: (p, 0, 0)),
        ],
        out_specs=pl.BlockSpec((pairs, block, d_block, width), lambda p: (0, p, 0, 0)),
        out_shape=jax.ShapeDtypeStruct((pairs, vectors, d_block, width), jnp.bfloat16),
        cost_estimate=pl.CostEstimate(
            flops=2 * pairs * d_block * c_block * vectors * width,
            bytes_accessed=2 * vectors * width * (c_block + pairs * d_block),
            transcendentals=0,
        ),
        name="halve",
    )(amplitudes.reshape(pairs * d_block, c_block), left_t)


def product(halved, block):
    pairs, vectors, d_block, width = halved.shape
    return jnp.einsum(
        "ika,kb->iab",
        halved.reshape(pairs, vectors * d_block, width),
        block.reshape(vectors * d_block, block.shape[2]),
        preferred_element_type=jnp.float32,
    )


class Reducer:
    def __init__(self):
        self.rows, self.cols, self.chols = (lax.axis_size(n) for n in ("row", "col", "chol"))
        self.duo = 2 if self.cols % 2 == 0 else 1
        self.col, self.chol = lax.axis_index("col"), lax.axis_index("chol")
        self.core = self.col % self.duo

    def swap(self, value):
        if self.duo == 1:
            return value
        return lax.ppermute(value, "col", [(q, q ^ 1) for q in range(self.cols)])

    def flat(self, row, col, chol):
        return (row * self.cols + col) * self.chols + chol

    def reduce(self, block, owner):
        pairs, width_a, width_b = block.shape
        half = width_a // self.duo
        mine = lax.dynamic_slice_in_dim(block, self.core * half, half, 1)
        if self.duo == 2:
            other = lax.dynamic_slice_in_dim(block, (1 - self.core) * half, half, 1)
            mine = mine + self.swap(other)
        mine = mine.reshape(self.chols, pairs // self.chols, half, width_b)
        low = mine.astype(jnp.bfloat16)
        groups = self.cols // self.duo
        total = None
        for dc in range(self.chols):
            part = lax.dynamic_index_in_dim(low, (self.chol - dc) % self.chols, 0, False)
            for dg in range(groups):
                if not (dc or dg):
                    continue
                perm = []
                for r in range(self.rows):
                    g = owner(r) // self.duo
                    for c in range(self.duo):
                        for h in range(self.chols):
                            perm.append((
                                self.flat(r, (g + dg) % groups * self.duo + c, (h + dc) % self.chols),
                                self.flat(r, g * self.duo + c, h)))
                got = lax.ppermute(part, ("row", "col", "chol"), perm).astype(jnp.float32)
                total = got if total is None else total + got
        here = lax.dynamic_index_in_dim(mine, self.chol, 0, False)
        total = here if total is None else here + total
        to = sum(jnp.where(lax.axis_index("row") == r, owner(r), 0) for r in range(self.rows))
        keep = jnp.where(to == self.col, total, 0.0)
        give = jnp.where(to == (self.col ^ 1 if self.duo == 2 else -1), total, 0.0)
        return keep, give

    def finish(self, keep, give):
        if self.duo == 1:
            return keep
        got = self.swap(give)
        first = self.core == 0
        return jnp.concatenate([jnp.where(first, keep, got), jnp.where(first, got, keep)], axis=1)


def gathered(left_vectors, right_vectors, amplitudes):
    columns = lax.axis_size("col")
    right_t = lax.all_gather(right_vectors, "row", axis=2, tiled=True).transpose(1, 0, 2)
    halved = halve(amplitudes, left_vectors.transpose(1, 0, 2))
    total = product(halved, right_t)
    pairs, width_a, width_b = total.shape
    total = total.reshape(pairs, width_a, columns, width_b // columns).transpose(2, 0, 1, 3)
    total = total.reshape(columns * pairs, width_a, width_b // columns)
    return lax.psum_scatter(total, ("col", "chol"), scatter_dimension=0, tiled=True)


def shards(left_vectors, right_vectors, amplitudes):
    return ladder_of(left_vectors, right_vectors, amplitudes)


def ladder_of(left_vectors, right_vectors, amplitudes):
    row = lax.axis_index("row")
    mate_pairs = ((0, 1), (1, 0), (2, 3), (3, 2))
    cross_pairs = ((1, 2), (2, 1))
    out_pairs = ((1, 0), (2, 3))
    inner = (row == 1) | (row == 2)
    owners = (lambda r: r, lambda r: r ^ 1, lambda r: 1 if r >= 2 else 2, lambda r: 0 if r >= 2 else 3)
    red = Reducer()

    def send(value, perm):
        return lax.ppermute(value, "row", perm)

    def reduce(block, owner):
        return red.reduce(block, owner)

    own = right_vectors.transpose(1, 0, 2)
    mate = send(own, mate_pairs)
    cross_in = send(own, cross_pairs)
    halved = halve(amplitudes, left_vectors.transpose(1, 0, 2))
    cross_out = send(cross_in, out_pairs)
    width_b = own.shape[2]
    cuts = [slice(0, 2 * LANES), slice(2 * LANES, width_b)]
    far_in = [send(mate[:, :, cut], cross_pairs) for cut in cuts]

    y_own = product(halved, own)
    y_mate = product(halved, mate)
    totals = [reduce(y_own, owners[0]), reduce(y_mate, owners[1])]
    far_out = [send(part, out_pairs) for part in far_in]
    y_cross = product(halved, jnp.where(inner, cross_in, cross_out))
    totals.append(reduce(y_cross, owners[2]))
    far = []
    for far_i, far_o in zip(far_in, far_out):
        y_far = product(halved, jnp.where(inner, far_i, far_o))
        far.append(reduce(y_far, owners[3]))
    keep, give = (sum(t[s] for t in totals) for s in range(2))
    outs = []
    for cut, (k, g) in zip(cuts, far):
        outs.append(red.finish(keep[:, :, cut] + k, give[:, :, cut] + g))
    return jnp.concatenate(outs, axis=2)


def solution(mesh):
    lined = mesh.shape["row"] == 4
    return jax.shard_map(
        shards if lined else gathered,
        mesh=mesh,
        in_specs=(P(None, ("col", "chol"), "row"), P(None, ("col", "chol"), "row"), P()),
        out_specs=P("chol", "row", "col"),
        check_vma=False,
    )
```

time: 782 us -> 634 us (0.81); the launches traced: 780 us -> 624 us
  waiting for transfers between devices: 477 us -> 257 us
  local copies, waits for them, and re-layouts: 150 us -> 66 us
  starting transfers between devices: 0.04 us -> 64.8 us
  Pallas kernels: 0 us -> 43.3 us
  other arithmetic: 0 us -> 30.3 us
  matrix products: 139 us -> 162 us
  between operations: 13.4 us -> 1.05 us
    all_gather x1 -> x0, waiting for transfers between devices: 352 us -> none  [shards(): right_full = lax.all_gather(right_vectors, 'row', axis=2, tiled=True)]
    ppermute x0 -> x29, waiting for transfers between devices: none -> 257 us  [the longest x7 212 us: send(): return lax.ppermute(value, 'row', perm)]
    reduce_scatter x1 -> x0, waiting for transfers between devices: 125 us -> none  [shards(): lax.psum_scatter(ladder, ('col', 'chol'), scatter_dimension=0, tiled=True)]
    reshape x2 -> x0, local copies, waits for them, and re-layouts: 97.3 us -> none  [the longest x1 50.1 us: shards(): halved = halved.reshape(pairs, d_block * vectors, width_a)]
    ppermute x0 -> x29, starting transfers between devices: none -> 64.8 us  [the longest x15 37.9 us: reduce(): got = lax.ppermute(part, ('row', 'col', 'chol'), perm).astype(jnp.float32)]
    pallas_call x0 -> x1, Pallas kernels: none -> 43.3 us  [halve(): pl.pallas_call(half_kernel, grid=(vectors // block,), in_specs=[pl.BlockS...]
    dot_general x2 -> x5, matrix products: 139 us -> 162 us  [product(): jnp.einsum('ika,kb->iab', halved.reshape(pairs, vectors * d_block, width)...]
    select_n x0 -> x5, other arithmetic: none -> 14.7 us  [the longest x1 6.69 us: ladder_of(): y_cross = product(halved, jnp.where(inner, cross_in, cross_out))]
  transfers between devices with their start and end apart: 2 -> 29, of which waited for: 2 -> 12; matrix products, arithmetic and copies ran while one was open for 17% -> 40% of each run, Pallas kernels for 0% -> 7%
where the time goes in v1:
time: 634 us; the launch traced here: 624 us
  waiting for transfers between devices  257 us (41%)
  matrix products  162 us (26%)
  local copies, waits for them, and re-layouts  66 us (10%)
  starting transfers between devices  64.8 us (10%)
  Pallas kernels  43.3 us (7%)
  other arithmetic  30.3 us (5%)
    ppermute x7, waiting for transfers between devices, send(): return lax.ppermute(value, 'row', perm)  212 us
    dot_general x5, matrix products, product(): jnp.einsum('ika,kb->iab', halved.reshape(pairs, vectors * d_block, width)...  162 us
    unnamed x23, local copies, waits for them, and re-layouts  49.6 us
    pallas_call x1, Pallas kernels, halve(): pl.pallas_call(half_kernel, grid=(vectors // block,), in_specs=[pl.BlockS...  43.3 us
    ppermute x15, waiting for transfers between devices, reduce(): got = lax.ppermute(part, ('row', 'col', 'chol'), perm).astype(jnp.float32)  42.2 us
    ppermute x15, starting transfers between devices, reduce(): got = lax.ppermute(part, ('row', 'col', 'chol'), perm).astype(jnp.float32)  37.9 us
    ppermute x7, starting transfers between devices, send(): return lax.ppermute(value, 'row', perm)  26.4 us
  transfers between devices with their start and end apart: 29, of which 12 were waited for; matrix products, arithmetic and copies ran while one was open for 40% of the time, Pallas kernels for 7%

profile of v1, /device:TPU:0, one launch (start us, length us, event | category | flops | bytes accessed | tf_op | source)
XLA Modules:
  0.0 623.9 jit_solution(11267000061951650875)
XLA Ops:
  0.0 3.1 collective-permute-start.4
  3.1 3.5 collective-permute-start.9
  6.6 44.0 %copy.46 = bf16[64,576,384]{2,0,1:T(8,128)(2,1)} copy(bf16[64,576,384]{2,1,0:T(8,128)(2,1)} %param.3) | data formatting | bytes 56623104 | tf_op args[0]
  50.6 43.3 %halve.1 = bf16[8,576,16,384]{3,2,1,0:T(8,128)(2,1)} custom-call(bf16[128,64]{1,0:T(8,128)(2,1)} %bitcast.94, bf16[576,64,384]{2,1,0:T(8,128)(2,1)} %bitcast.83), custom_call_target="tpu_custom_call" | custom-call | flops 3623878656 | bytes 84934656 | tf_op jit(solution)/shard_map/halve/pallas_call | solution.py:24
  93.9 38.3 %fusion.10 = f32[8,384,384]{2,1,0:T(8,128)S(1)} fusion(bf16[8,576,16,384]{3,2,1,0:T(8,128)(2,1)} %halve.1, bf16[576,16,384,1]{2,0,1,3:T(8,128)(2,1)} %bitcast.97), kind=kOutput, calls=%fused_computation.18 | convolution fusion | flops 21743271936 | bytes 68419584 | tf_op jit(solution)/shard_map/ika,kb->iab/dot_general | solution.py:44
  135.1 20.6 %collective-permute-done.4 = bf16[576,16,384]{2,0,1:T(8,128)(2,1)} collective-permute-done((bf16[576,16,384]{2,0,1:T(8,128)(2,1)}, bf16[576,16,384]{2,0,1:T(8,128)(2,1)}, u32[]{:S(2)}, u32[]{:S(2)}) %collective-permute-start.4) | collective-permute-done | bytes 7077920 | tf_op jit(solution)/shard_map/ppermute | solution.py:133
  155.7 3.2 slice.28
  161.1 2.6 dynamic-slice_add_fusion.2
  166.9 3.6 collective-permute-start.2
  170.5 2.7 slice.25
  173.1 3.0 collective-permute-start.15
  176.1 13.4 %collective-permute-start.23 = (bf16[576,16,128]{2,0,1:T(8,128)(2,1)S(1)}, bf16[576,16,128]{2,0,1:T(8,128)(2,1)S(1)}, u32[]{:S(2)}, u32[]{:S(2)}) collective-permute-start(bf16[576,16,128]{2,0,1:T(8,128)(2,1)S(1)} %collective-permute-done.22), channel_id=1, source_target_pairs={{8,0},{16,24},{9,1},{17,25},{10,2},{18,26},{11,3},{19,27},{12,4},{... | collective-permute-start | bytes 7077896 | tf_op jit(solution)/shard_map/ppermute | solution.py:133
  189.5 38.3 %fusion.13 = f32[8,384,384]{2,1,0:T(8,128)S(1)} fusion(bf16[8,576,16,384]{3,2,1,0:T(8,128)(2,1)} %halve.1, bf16[576,16,384,1]{2,0,1,3:T(8,128)(2,1)} %bitcast.10), kind=kOutput, calls=%fused_computation.19 | convolution fusion | flops 21743271936 | bytes 68419584 | tf_op jit(solution)/shard_map/ika,kb->iab/dot_general | solution.py:44
  230.7 136.7 %collective-permute-done.23 = bf16[576,16,128]{2,0,1:T(8,128)(2,1)S(1)} collective-permute-done((bf16[576,16,128]{2,0,1:T(8,128)(2,1)S(1)}, bf16[576,16,128]{2,0,1:T(8,128)(2,1)S(1)}, u32[]{:S(2)}, u32[]{:S(2)}) %collective-permute-start.23) | collective-permute-done | bytes 2359328 | tf_op jit(solution)/shard_map/ppermute | solution.py:133
  370.5 6.7 %select_bitcast_fusion = bf16[576,16,384,1]{2,0,1,3:T(8,128)(2,1)} fusion(bf16[576,16,384]{2,0,1:T(8,128)(2,1)} %collective-permute-done.9, bf16[576,16,384]{2,0,1:T(8,128)(2,1)} %collective-permute-done.10, pred[]{:T(512)S(6)} %or.3), kind=kLoop, calls=%fused_computation.7 | loop fusion | flops 3538944 | bytes 21233664 | tf_op jit(solution)/shard_map/jit(_where)/select_n | solution.py:151
  377.2 38.3 %fusion.16 = f32[8,384,384]{2,1,0:T(8,128)S(1)} fusion(bf16[8,576,16,384]{3,2,1,0:T(8,128)(2,1)} %halve.1, bf16[576,16,384,1]{2,0,1,3:T(8,128)(2,1)} %select_bitcast_fusion), kind=kOutput, calls=%fused_computation.20 | convolution fusion | flops 21743271936 | bytes 68419584 | tf_op jit(solution)/shard_map/ika,kb->iab/dot_general | solution.py:44
  418.8 55.1 %collective-permute-done.16 = bf16[576,16,256]{2,0,1:T(8,128)(2,1)} collective-permute-done((bf16[576,16,256]{2,0,1:T(8,128)(2,1)}, bf16[576,16,256]{2,0,1:T(8,128)(2,1)}, u32[]{:S(2)}, u32[]{:S(2)}) %collective-permute-start.16) | collective-permute-done | bytes 4718624 | tf_op jit(solution)/shard_map/ppermute | solution.py:133
  473.9 4.9 select_bitcast_fusion.1
  478.8 24.2 %fusion.19 = f32[8,384,256]{2,1,0:T(8,128)S(1)} fusion(bf16[8,576,16,384]{3,2,1,0:T(8,128)(2,1)} %halve.1, bf16[576,16,256,1]{2,0,1,3:T(8,128)(2,1)} %select_bitcast_fusion.1), kind=kOutput, calls=%fused_computation.21 | convolution fusion | flops 14495514624 | bytes 64487424 | tf_op jit(solution)/shard_map/ika,kb->iab/dot_general | solution.py:44
  506.4 22.7 %fusion.22 = f32[8,384,128]{2,1,0:T(8,128)S(1)} fusion(bf16[8,576,16,384]{3,2,1,0:T(8,128)(2,1)} %halve.1, bf16[576,16,128,1]{2,0,1,3:T(8,128)(2,1)S(1)} %copy-done.7), kind=kOutput, calls=%fused_computation.23 | convolution fusion | flops 7247757312 | bytes 60555264 | tf_op jit(solution)/shard_map/ika,kb->iab/dot_general | solution.py:44
  530.2 2.6 dynamic-slice_add_fusion.1
  539.8 3.7 collective-permute-start.7
  543.5 9.1 %collective-permute-done.1 = bf16[4,192,384]{2,1,0:T(8,128)(2,1)} collective-permute-done((bf16[4,192,384]{2,1,0:T(8,128)(2,1)}, bf16[4,192,384]{2,1,0:T(8,128)(2,1)}, u32[]{:S(2)}, u32[]{:S(2)}) %collective-permute-start.1) | collective-permute-done | bytes 589856 | tf_op jit(solution)/shard_map/ppermute | solution.py:91
  553.9 12.4 %collective-permute-done.8 = bf16[4,192,384]{2,1,0:T(8,128)(2,1)} collective-permute-done((bf16[4,192,384]{2,1,0:T(8,128)(2,1)}, bf16[4,192,384]{2,1,0:T(8,128)(2,1)}, u32[]{:S(2)}, u32[]{:S(2)}) %collective-permute-start.8) | collective-permute-done | bytes 589856 | tf_op jit(solution)/shard_map/ppermute | solution.py:91
  568.4 3.1 collective-permute-start.12
  578.0 3.4 collective-permute-done.14
  581.4 5.3 collective-permute-start.20
  587.4 6.6 %collective-permute-done.12 = bf16[4,192,384]{2,1,0:T(8,128)(2,1)S(1)} collective-permute-done((bf16[4,192,384]{2,1,0:T(8,128)(2,1)S(1)}, bf16[4,192,384]{2,1,0:T(8,128)(2,1)S(1)}, u32[]{:S(2)}, u32[]{:S(2)}) %collective-permute-start.12) | collective-permute-done | bytes 589856 | tf_op jit(solution)/shard_map/ppermute | solution.py:91
  594.1 7.8 %collective-permute-start.18 = (bf16[4,192,256]{2,1,0:T(8,128)(2,1)S(1)}, bf16[4,192,256]{2,1,0:T(8,128)(2,1)S(1)}, u32[]{:S(2)}, u32[]{:S(2)}) collective-permute-start(bf16[4,192,256]{2,1,0:T(8,128)(2,1)S(1)} %get-tuple-element.21), channel_id=1, source_target_pairs={{0,4},{1,5},{2,6},{3,7},{8,12},{9,13},{10,14},{11,15},{20,16},{21,... | collective-permute-start | bytes 1179656 | tf_op jit(solution)/shard_map/ppermute | solution.py:91
  601.9 2.7 select_add_fusion.1
  606.7 4.3 collective-permute-start.25
  611.1 4.1 collective-permute-done.18
  (86 shorter events, 49.4 us)
Async XLA Ops:
  0.0 155.7 %collective-permute-start.4 = (bf16[576,16,384]{2,0,1:T(8,128)(2,1)}, bf16[576,16,384]{2,0,1:T(8,128)(2,1)}, u32[]{:S(2)}, u32[]{:S(2)}) collective-permute-start(bf16[576,16,384]{2,0,1:T(8,128)(2,1)} %bitcast.95), channel_id=1, source_target_pairs={{0,8},{8,0},{16,24},{24,16},{1,9},{9,1},{17,25},{25,17},{2,10},{10... | collective-permute-start | bytes 21233672 | tf_op jit(solution)/shard_map/ppermute | solution.py:133
  3.1 156.7 %collective-permute-start.9 = (bf16[576,16,384]{2,0,1:T(8,128)(2,1)}, bf16[576,16,384]{2,0,1:T(8,128)(2,1)}, u32[]{:S(2)}, u32[]{:S(2)}) collective-permute-start(bf16[576,16,384]{2,0,1:T(8,128)(2,1)} %bitcast.96), channel_id=1, source_target_pairs={{8,16},{16,8},{9,17},{17,9},{10,18},{18,10},{11,19},{19,11},{12,20... | collective-permute-start | bytes 21233672 | tf_op jit(solution)/shard_map/ppermute | solution.py:133
  135.1 26.0 %collective-permute-start = (f32[8,192,384]{2,1,0:T(8,128)}, f32[8,192,384]{2,1,0:T(8,128)}, u32[]{:S(2)}, u32[]{:S(2)}) collective-permute-start(f32[8,192,384]{2,1,0:T(8,128)} %constant_dynamic-slice_fusion.4), channel_id=1, source_target_pairs={{0,2},{2,0},{4,6},{6,4},{1,3},{3,1},{5,7},{7,5},{8,10},{10,8},{12,... | collective-permute-start | bytes 7077896 | tf_op jit(solution)/shard_map/ppermute | solution.py:62
  159.0 17.1 %collective-permute-start.22 = (bf16[576,16,128]{2,0,1:T(8,128)(2,1)}, bf16[576,16,128]{2,0,1:T(8,128)(2,1)S(1)}, u32[]{:S(2)}, u32[]{:S(2)}) collective-permute-start(bf16[576,16,128]{2,0,1:T(8,128)(2,1)} %slice.28), channel_id=1, source_target_pairs={{8,16},{16,8},{9,17},{17,9},{10,18},{18,10},{11,19},{19,11},{12,20... | collective-permute-start | bytes 7077896 | tf_op jit(solution)/shard_map/ppermute | solution.py:133
  159.8 210.7 %collective-permute-start.10 = (bf16[576,16,384]{2,0,1:T(8,128)(2,1)}, bf16[576,16,384]{2,0,1:T(8,128)(2,1)}, u32[]{:S(2)}, u32[]{:S(2)}) collective-permute-start(bf16[576,16,384]{2,0,1:T(8,128)(2,1)} %collective-permute-done.9), channel_id=1, source_target_pairs={{8,0},{16,24},{9,1},{17,25},{10,2},{18,26},{11,3},{19,27},{12,4},{... | collective-permute-start | bytes 21233672 | tf_op jit(solution)/shard_map/ppermute | solution.py:133
  165.6 368.6 %collective-permute-start.3 = (bf16[4,192,384]{2,1,0:T(8,128)(2,1)}, bf16[4,192,384]{2,1,0:T(8,128)(2,1)}, u32[]{:S(2)}, u32[]{:S(2)}) collective-permute-start(bf16[4,192,384]{2,1,0:T(8,128)(2,1)} %get-tuple-element.20), channel_id=1, source_target_pairs={{5,0},{4,1},{7,2},{6,3},{13,8},{12,9},{15,10},{14,11},{17,20},{16,... | collective-permute-start | bytes 1769480 | tf_op jit(solution)/shard_map/ppermute | solution.py:91
  166.9 372.9 %collective-permute-start.2 = (bf16[4,192,384]{2,1,0:T(8,128)(2,1)}, bf16[4,192,384]{2,1,0:T(8,128)(2,1)}, u32[]{:S(2)}, u32[]{:S(2)}) collective-permute-start(bf16[4,192,384]{2,1,0:T(8,128)(2,1)} %get-tuple-element.20), channel_id=1, source_target_pairs={{1,0},{0,1},{3,2},{2,3},{9,8},{8,9},{11,10},{10,11},{21,20},{20,21... | collective-permute-start | bytes 1769480 | tf_op jit(solution)/shard_map/ppermute | solution.py:91
  173.1 194.4 %collective-permute-start.15 = (bf16[576,16,256]{2,0,1:T(8,128)(2,1)S(1)}, bf16[576,16,256]{2,0,1:T(8,128)(2,1)}, u32[]{:S(2)}, u32[]{:S(2)}) collective-permute-start(bf16[576,16,256]{2,0,1:T(8,128)(2,1)S(1)} %slice.25), channel_id=1, source_target_pairs={{8,16},{16,8},{9,17},{17,9},{10,18},{18,10},{11,19},{19,11},{12,20... | collective-permute-start | bytes 14155784 | tf_op jit(solution)/shard_map/ppermute | solution.py:133
  176.1 191.4 %collective-permute-start.23 = (bf16[576,16,128]{2,0,1:T(8,128)(2,1)S(1)}, bf16[576,16,128]{2,0,1:T(8,128)(2,1)S(1)}, u32[]{:S(2)}, u32[]{:S(2)}) collective-permute-start(bf16[576,16,128]{2,0,1:T(8,128)(2,1)S(1)} %collective-permute-done.22), channel_id=1, source_target_pairs={{8,0},{16,24},{9,1},{17,25},{10,2},{18,26},{11,3},{19,27},{12,4},{... | collective-permute-start | bytes 7077896 | tf_op jit(solution)/shard_map/ppermute | solution.py:133
  367.5 162.7 %collective-permute-start.5 = (f32[8,192,384]{2,1,0:T(8,128)}, f32[8,192,384]{2,1,0:T(8,128)}, u32[]{:S(2)}, u32[]{:S(2)}) collective-permute-start(f32[8,192,384]{2,1,0:T(8,128)} %constant_dynamic-slice_fusion.3), channel_id=1, source_target_pairs={{0,2},{2,0},{4,6},{6,4},{1,3},{3,1},{5,7},{7,5},{8,10},{10,8},{12,... | collective-permute-start | bytes 7077896 | tf_op jit(solution)/shard_map/ppermute | solution.py:62
  367.5 106.4 %collective-permute-start.16 = (bf16[576,16,256]{2,0,1:T(8,128)(2,1)}, bf16[576,16,256]{2,0,1:T(8,128)(2,1)}, u32[]{:S(2)}, u32[]{:S(2)}) collective-permute-start(bf16[576,16,256]{2,0,1:T(8,128)(2,1)} %collective-permute-done.15), channel_id=1, source_target_pairs={{8,0},{16,24},{9,1},{17,25},{10,2},{18,26},{11,3},{19,27},{12,4},{... | collective-permute-start | bytes 14155784 | tf_op jit(solution)/shard_map/ppermute | solution.py:133
  418.3 117.1 %collective-permute-start.11 = (f32[8,192,384]{2,1,0:T(8,128)}, f32[8,192,384]{2,1,0:T(8,128)}, u32[]{:S(2)}, u32[]{:S(2)}) collective-permute-start(f32[8,192,384]{2,1,0:T(8,128)} %constant_dynamic-slice_fusion.2), channel_id=1, source_target_pairs={{0,2},{2,0},{4,6},{6,4},{1,3},{3,1},{5,7},{7,5},{8,10},{10,8},{12,... | collective-permute-start | bytes 7077896 | tf_op jit(solution)/shard_map/ppermute | solution.py:62
  504.4 64.1 %collective-permute-start.17 = (f32[8,192,256]{2,1,0:T(8,128)}, f32[8,192,256]{2,1,0:T(8,128)}, u32[]{:S(2)}, u32[]{:S(2)}) collective-permute-start(f32[8,192,256]{2,1,0:T(8,128)} %constant_dynamic-slice_fusion.1), channel_id=1, source_target_pairs={{0,2},{2,0},{4,6},{6,4},{1,3},{3,1},{5,7},{7,5},{8,10},{10,8},{12,... | collective-permute-start | bytes 4718600 | tf_op jit(solution)/shard_map/ppermute | solution.py:62
  530.2 37.5 %collective-permute-start.24 = (f32[8,192,128]{2,1,0:T(8,128)}, f32[8,192,128]{2,1,0:T(8,128)S(1)}, u32[]{:S(2)}, u32[]{:S(2)}) collective-permute-start(f32[8,192,128]{2,1,0:T(8,128)} %constant_dynamic-slice_fusion), channel_id=1, source_target_pairs={{0,2},{2,0},{4,6},{6,4},{1,3},{3,1},{5,7},{7,5},{8,10},{10,8},{12,... | collective-permute-start | bytes 2359304 | tf_op jit(solution)/shard_map/ppermute | solution.py:62
  534.2 18.4 %collective-permute-start.1 = (bf16[4,192,384]{2,1,0:T(8,128)(2,1)}, bf16[4,192,384]{2,1,0:T(8,128)(2,1)}, u32[]{:S(2)}, u32[]{:S(2)}) collective-permute-start(bf16[4,192,384]{2,1,0:T(8,128)(2,1)} %get-tuple-element.19), channel_id=1, source_target_pairs={{4,0},{5,1},{6,2},{7,3},{12,8},{13,9},{14,10},{15,11},{16,20},{17,... | collective-permute-start | bytes 1769480 | tf_op jit(solution)/shard_map/ppermute | solution.py:91
  535.5 30.7 %collective-permute-start.8 = (bf16[4,192,384]{2,1,0:T(8,128)(2,1)}, bf16[4,192,384]{2,1,0:T(8,128)(2,1)}, u32[]{:S(2)}, u32[]{:S(2)}) collective-permute-start(bf16[4,192,384]{2,1,0:T(8,128)(2,1)} %get-tuple-element.18), channel_id=1, source_target_pairs={{5,0},{4,1},{7,2},{6,3},{13,8},{12,9},{15,10},{14,11},{17,20},{16,... | collective-permute-start | bytes 1769480 | tf_op jit(solution)/shard_map/ppermute | solution.py:91
  539.5 32.0 %copy-start.9 = (f32[8,384,128]{2,1,0:T(8,128)S(1)}, f32[8,384,128]{2,1,0:T(8,128)}, u32[]{:S(2)}) copy-start(f32[8,384,128]{2,1,0:T(8,128)} %copy-done.8) | copy-start | bytes 4718596
  539.8 32.0 %copy-start.6 = (f32[8,384,256]{2,1,0:T(8,128)S(1)}, f32[8,384,256]{2,1,0:T(8,128)}, u32[]{:S(2)}) copy-start(f32[8,384,256]{2,1,0:T(8,128)} %copy-done.5) | copy-start | bytes 9437188
  539.8 33.8 %collective-permute-start.7 = (bf16[4,192,384]{2,1,0:T(8,128)(2,1)}, bf16[4,192,384]{2,1,0:T(8,128)(2,1)S(1)}, u32[]{:S(2)}, u32[]{:S(2)}) collective-permute-start(bf16[4,192,384]{2,1,0:T(8,128)(2,1)} %get-tuple-element.18), channel_id=1, source_target_pairs={{1,0},{0,1},{3,2},{2,3},{9,8},{8,9},{11,10},{10,11},{21,20},{20,21... | collective-permute-start | bytes 1769480 | tf_op jit(solution)/shard_map/ppermute | solution.py:91
  552.6 24.8 %collective-permute-start.6 = (bf16[4,192,384]{2,1,0:T(8,128)(2,1)S(1)}, bf16[4,192,384]{2,1,0:T(8,128)(2,1)S(1)}, u32[]{:S(2)}, u32[]{:S(2)}) collective-permute-start(bf16[4,192,384]{2,1,0:T(8,128)(2,1)S(1)} %copy-done.10), channel_id=1, source_target_pairs={{4,0},{5,1},{6,2},{7,3},{12,8},{13,9},{14,10},{15,11},{16,20},{17,... | collective-permute-start | bytes 1769480 | tf_op jit(solution)/shard_map/ppermute | solution.py:91
  566.2 15.2 %collective-permute-start.14 = (bf16[4,192,384]{2,1,0:T(8,128)(2,1)S(1)}, bf16[4,192,384]{2,1,0:T(8,128)(2,1)S(1)}, u32[]{:S(2)}, u32[]{:S(2)}) collective-permute-start(bf16[4,192,384]{2,1,0:T(8,128)(2,1)S(1)} %get-tuple-element.16), channel_id=1, source_target_pairs={{1,4},{0,5},{3,6},{2,7},{9,12},{8,13},{11,14},{10,15},{21,16},{20,... | collective-permute-start | bytes 1769480 | tf_op jit(solution)/shard_map/ppermute | solution.py:91
  567.7 19.0 %collective-permute-start.13 = (bf16[4,192,384]{2,1,0:T(8,128)(2,1)S(1)}, bf16[4,192,384]{2,1,0:T(8,128)(2,1)S(1)}, u32[]{:S(2)}, u32[]{:S(2)}) collective-permute-start(bf16[4,192,384]{2,1,0:T(8,128)(2,1)S(1)} %get-tuple-element.16), channel_id=1, source_target_pairs={{5,4},{4,5},{7,6},{6,7},{13,12},{12,13},{15,14},{14,15},{17,16},{1... | collective-permute-start | bytes 1769480 | tf_op jit(solution)/shard_map/ppermute | solution.py:91
  568.4 25.6 %collective-permute-start.12 = (bf16[4,192,384]{2,1,0:T(8,128)(2,1)S(1)}, bf16[4,192,384]{2,1,0:T(8,128)(2,1)S(1)}, u32[]{:S(2)}, u32[]{:S(2)}) collective-permute-start(bf16[4,192,384]{2,1,0:T(8,128)(2,1)S(1)} %get-tuple-element.15), channel_id=1, source_target_pairs={{0,4},{1,5},{2,6},{3,7},{8,12},{9,13},{10,14},{11,15},{20,16},{21,... | collective-permute-start | bytes 1769480 | tf_op jit(solution)/shard_map/ppermute | solution.py:91
  573.4 28.5 %copy-start.1 = (f32[8,192,384]{2,1,0:T(8,128)S(1)}, f32[8,192,384]{2,1,0:T(8,128)}, u32[]{:S(2)}) copy-start(f32[8,192,384]{2,1,0:T(8,128)} %copy-done) | copy-start | bytes 7077892
  573.6 41.9 %collective-permute-start.27 = (bf16[4,192,128]{2,1,0:T(8,128)(2,1)S(1)}, bf16[4,192,128]{2,1,0:T(8,128)(2,1)S(1)}, u32[]{:S(2)}, u32[]{:S(2)}) collective-permute-start(bf16[4,192,128]{2,1,0:T(8,128)(2,1)S(1)} %get-tuple-element.24), channel_id=1, source_target_pairs={{1,4},{0,5},{3,6},{2,7},{9,12},{8,13},{11,14},{10,15},{21,16},{20,... | collective-permute-start | bytes 589832 | tf_op jit(solution)/shard_map/ppermute | solution.py:91
  577.3 38.1 %collective-permute-start.26 = (bf16[4,192,128]{2,1,0:T(8,128)(2,1)S(1)}, bf16[4,192,128]{2,1,0:T(8,128)(2,1)S(1)}, u32[]{:S(2)}, u32[]{:S(2)}) collective-permute-start(bf16[4,192,128]{2,1,0:T(8,128)(2,1)S(1)} %get-tuple-element.24), channel_id=1, source_target_pairs={{5,4},{4,5},{7,6},{6,7},{13,12},{12,13},{15,14},{14,15},{17,16},{1... | collective-permute-start | bytes 589832 | tf_op jit(solution)/shard_map/ppermute | solution.py:91
  581.4 25.3 %collective-permute-start.20 = (bf16[4,192,256]{2,1,0:T(8,128)(2,1)S(1)}, bf16[4,192,256]{2,1,0:T(8,128)(2,1)S(1)}, u32[]{:S(2)}, u32[]{:S(2)}) collective-permute-start(bf16[4,192,256]{2,1,0:T(8,128)(2,1)S(1)} %get-tuple-element.22), channel_id=1, source_target_pairs={{1,4},{0,5},{3,6},{2,7},{9,12},{8,13},{11,14},{10,15},{21,16},{20,... | collective-permute-start | bytes 1179656 | tf_op jit(solution)/shard_map/ppermute | solution.py:91
  586.7 24.3 %collective-permute-start.19 = (bf16[4,192,256]{2,1,0:T(8,128)(2,1)S(1)}, bf16[4,192,256]{2,1,0:T(8,128)(2,1)S(1)}, u32[]{:S(2)}, u32[]{:S(2)}) collective-permute-start(bf16[4,192,256]{2,1,0:T(8,128)(2,1)S(1)} %get-tuple-element.22), channel_id=1, source_target_pairs={{5,4},{4,5},{7,6},{6,7},{13,12},{12,13},{15,14},{14,15},{17,16},{1... | collective-permute-start | bytes 1179656 | tf_op jit(solution)/shard_map/ppermute | solution.py:91
  594.1 21.1 %collective-permute-start.18 = (bf16[4,192,256]{2,1,0:T(8,128)(2,1)S(1)}, bf16[4,192,256]{2,1,0:T(8,128)(2,1)S(1)}, u32[]{:S(2)}, u32[]{:S(2)}) collective-permute-start(bf16[4,192,256]{2,1,0:T(8,128)(2,1)S(1)} %get-tuple-element.21), channel_id=1, source_target_pairs={{0,4},{1,5},{2,6},{3,7},{8,12},{9,13},{10,14},{11,15},{20,16},{21,... | collective-permute-start | bytes 1179656 | tf_op jit(solution)/shard_map/ppermute | solution.py:91
  606.7 11.0 %collective-permute-start.25 = (bf16[4,192,128]{2,1,0:T(8,128)(2,1)S(1)}, bf16[4,192,128]{2,1,0:T(8,128)(2,1)S(1)}, u32[]{:S(2)}, u32[]{:S(2)}) collective-permute-start(bf16[4,192,128]{2,1,0:T(8,128)(2,1)S(1)} %get-tuple-element.23), channel_id=1, source_target_pairs={{0,4},{1,5},{2,6},{3,7},{8,12},{9,13},{10,14},{11,15},{20,16},{21,... | collective-permute-start | bytes 589832 | tf_op jit(solution)/shard_map/ppermute | solution.py:91
  615.4 5.2 collective-permute-start.21
  618.6 1.9 collective-permute-start.28
  (8 other events, 56.7 us)
